TPU v7x, 512 devices: a whole 4x8x8 slice. The times are simulated.
512 devices in a mesh: seq: 128 (over z, y, core), grp: 4 (over x).
Axes of the slice: x: 4, y: 8, z: 8, core: 2. Of those that a mesh axis runs over, the one named last changes fastest.
Arguments:
- frames: bfloat16 [262144, 1024], P(('seq', 'grp')), may hold values from -6 to 6
- ln1_gain: float32 [1024], replicated, may hold values from 0.1 to 1.9
- w_in: bfloat16 [1024, 2, 1024], P('seq', None, 'grp'), may hold values from -0.1875 to 0.1875
- w_dw: bfloat16 [31, 1024], replicated, may hold values from -1 to 1
- ln2_gain: float32 [1024], replicated, may hold values from 0.1 to 1.9
- ln2_bias: float32 [1024], replicated, may hold values from -3 to 3
- w_out: bfloat16 [1024, 1024], P('grp', 'seq'), may hold values from -0.1875 to 0.1875
- block_utt: int32 [2048], replicated, may hold values from 0 to 511, as said below
- block_off: int32 [2048], replicated, may hold values from 0 to 6, as said below
- lengths: int32 [512], replicated, may hold values from 1 to 896, as said below
Outputs:
- result: bfloat16 [262144, 1024], P(('seq', 'grp'))
Inputs may be any that keep to these rules, and one draw needn't show every extreme that they name: block_utt never falls along the blocks and names every utterance; each utterance is one run of 1 to 7 whole blocks, and some utterance has exactly 7. block_off counts the blocks of the run before a block, starting at 0. `lengths`: an utterance of n blocks has more than (n - 1) * 128 and at most n * 128 live frames.
All inputs are finite; a program needn't handle non-finite values.
Results may differ from a plain program's by a relative error of at most 0.0046.
Values may be sent and summed in bfloat16 or wider, within the bound.
No kernel may reach another device: no remote copies, remote signals or barrier semaphores. Data moves between devices by JAX's collectives and lax.ppermute only.
A program may use at most 64 MiB of HBM per device.

v0:
```python
import jax
import jax.numpy as jnp
from jax import lax
from jax.sharding import Mesh
from jax.sharding import PartitionSpec as P

D = 1024
KER = 31
BLK = 128
SEQ_GRP = ("seq_0", "seq_1", "seq_2", "grp")
SEQ = ("seq_0", "seq_1", "seq_2")


epsilon = 1e-05


def turned_gather(arrays, axis, dims):
    turned = [jnp.moveaxis(a, dim, 0) for a, dim in zip(arrays, dims)]
    both = jnp.concatenate([t.reshape(len(t), -1) for t in turned], axis=1)
    whole, at, finished = (lax.all_gather(both, axis, axis=0, tiled=True), 0, [])
    for t, dim in zip(turned, dims):
        section = whole[:, at : at + t[0].size].reshape(-1, *t.shape[1:])
        finished.append(jnp.moveaxis(section, 0, dim))
        at += t[0].size
    return tuple(finished)


def sent_to_all(array, axis):
    size = lax.axis_size(axis)
    return lax.all_to_all(
        jnp.broadcast_to(array[None], (size, *array.shape)), axis, 0, 0, tiled=True
    )


def joined_along(pieces, dim):
    dims = list(pieces.shape[1:])
    dims[dim] *= pieces.shape[0]
    return jnp.moveaxis(pieces, 0, dim).reshape(dims)


def gather_axes(array, axes, dim):
    far, near = axes
    pieces = sent_to_all(sent_to_all(array, far), near)
    return joined_along(pieces.swapaxes(0, 1).reshape(-1, *array.shape), dim)


def extended(array, sides, width):
    edges = {}
    for axis, dim in sides:
        size, length = (lax.axis_size(axis), array.shape[dim])
        up = [(i, (i + 1) % size) for i in range(size - 1)]
        last = lax.slice_in_dim(array, length - width, length, axis=dim)
        leading = lax.slice_in_dim(array, 0, width, axis=dim)
        edges[dim] = (
            lax.ppermute(last, axis, up),
            lax.ppermute(leading, axis, [(b, a) for a, b in up]),
        )
    done = []
    for _, dim in sides:
        low, high = edges[dim]
        around = [(width, width) if d in done else (0, 0) for d in range(array.ndim)]
        array = jnp.concatenate([jnp.pad(low, around), array, jnp.pad(high, around)], axis=dim)
        done.append(dim)
    return array


def frame_keys(block_utt, block_off, lengths, first_row, row_count, margin):
    places = first_row - margin + jnp.arange(row_count + 2 * margin, dtype=jnp.int32)
    total_rows = block_utt.shape[0] * BLK
    inside = (places >= 0) & (places < total_rows)
    blocks = jnp.clip(places // BLK, 0, block_utt.shape[0] - 1)
    utterance = jnp.take(block_utt, blocks)
    position = jnp.take(block_off, blocks) * BLK + places % BLK
    living = inside & (position < jnp.take(lengths, utterance))
    return (jnp.where(living, utterance, -1), living[margin : margin + row_count])


def layer_norm(rows, gain):
    values = rows.astype(jnp.float32)
    average = jnp.mean(values, axis=1, keepdims=True)
    centered = values - average
    spread = jnp.mean(centered * centered, axis=1, keepdims=True)
    return (centered * lax.rsqrt(spread + epsilon) * gain).astype(jnp.bfloat16)


def gate_units(projected, living):
    half = projected.shape[1] // 2
    values = projected[:, :half] * jax.nn.sigmoid(projected[:, half:])
    return (values * living.astype(jnp.float32)[:, None]).astype(jnp.bfloat16)


def depthwise(widened, keys_wide, taps, row_count):
    margin = (taps.shape[0] - 1) // 2
    center = keys_wide[margin : margin + row_count]
    summed = jnp.zeros((row_count, widened.shape[1]), jnp.float32)
    for tap_index in range(taps.shape[0]):
        shifted = widened[tap_index : tap_index + row_count].astype(jnp.float32)
        same = (keys_wide[tap_index : tap_index + row_count] == center)[:, None]
        summed = summed + jnp.where(same, shifted, 0.0) * taps[tap_index].astype(jnp.float32)
    return summed


def finish(mixed, stat_sum, square_sum, width_total, gain, bias):
    average = stat_sum / width_total
    spread = square_sum / width_total - average * average
    normed = (mixed - average[:, None]) * lax.rsqrt(spread + epsilon)[:, None] * gain + bias
    return (normed * jax.nn.sigmoid(normed)).astype(jnp.bfloat16)


def project_rows(normed, row_count, column_count):

    def add_rows(total, weight_piece, start_row):
        piece_rows = weight_piece.shape[0]
        return jnp.dot(
            normed, weight_piece.reshape(piece_rows, -1), preferred_element_type=jnp.float32
        )

    return (add_rows, jnp.zeros((row_count, column_count), jnp.float32))


def per_device(
    frames, ln1_gain, w_in, w_dw, ln2_gain, ln2_bias, w_out, block_utt, block_off, lengths
):
    row_count = frames.shape[0]
    margin = (KER - 1) // 2
    own_first = lax.axis_index(SEQ_GRP) * row_count
    keys_wide, living = frame_keys(block_utt, block_off, lengths, own_first, row_count, margin)
    normed = layer_norm(frames, ln1_gain)
    w_in_rows, w_out_rows = turned_gather((w_in, w_out), "grp", (2, 0))
    add_rows, empty = project_rows(normed, row_count, 2 * D)
    projected = add_rows(
        empty, gather_axes(w_in_rows, (("seq_0", "seq_1"), "seq_2"), 0), jnp.int32(0)
    )
    gated = gate_units(projected, living)
    widened = extended(gated, ((SEQ_GRP, 0),), margin)
    mixed = depthwise(widened, keys_wide, w_dw, row_count)
    act = finish(
        mixed, jnp.sum(mixed, axis=1), jnp.sum(mixed * mixed, axis=1), float(D), ln2_gain, ln2_bias
    )
    output = jnp.dot(
        act, lax.all_gather(w_out_rows, SEQ, axis=1, tiled=True), preferred_element_type=jnp.float32
    )
    alive = living.astype(jnp.float32)[:, None]
    return (frames.astype(jnp.float32) + output * alive).astype(jnp.bfloat16)


def solution(mesh):
    finer = Mesh(
        mesh.devices.reshape(8, 8, 2, mesh.shape["grp"]), ("seq_0", "seq_1", "seq_2", "grp")
    )
    in_specs = (
        P(SEQ_GRP, None),
        P(),
        P(SEQ, None, "grp"),
        P(),
        P(),
        P(),
        P("grp", SEQ),
        P(),
        P(),
        P(),
    )
    out_specs = P(SEQ_GRP, None)
    return jax.shard_map(
        per_device, mesh=finer, in_specs=in_specs, out_specs=out_specs, check_vma=False
    )
```

profile of v0, /device:TPU:63, one launch (start us, length us, event | category | flops | bytes accessed | tf_op | source)
XLA Modules:
  0.0 159.7 jit_solution(3964374576333147791)
XLA Ops:
  6.5 0.0 copy-start
  6.5 0.7 reshape.76
  7.3 0.7 pad_maximum_fusion.2
  7.9 9.0 %all_gather.6 = bf16[1024,24]{0,1:T(8,128)(2,1)S(1)} all-gather(bf16[256,24]{0,1:T(8,128)(2,1)S(1)} %pad_maximum_fusion.2), channel_id=1, replica_groups=mesh['seq_0'=8,'seq_1'=8,'seq_2'=2,'grp'=4] {'grp'}, dimensions={0}, use_global_device_ids=true | all-gather | bytes 61440 | tf_op jit(solution)/shard_map/all_gather | solution.py:20
  17.0 3.4 %broadcast_in_dim.292 = bf16[64,8,2,1024]{3,2,1,0:T(2,128)(2,1)} broadcast(bf16[8,2,1024]{2,1,0:T(2,128)(2,1)S(1)} %bitcast.46), dimensions={1,2,3} | broadcast | bytes 2129920 | tf_op jit(solution)/shard_map/broadcast_in_dim | solution.py:31
  20.3 15.3 %all-to-all-start = ((bf16[64,8,2,1024]{3,2,1,0:T(2,128)(2,1)}), bf16[64,8,2,1024]{3,2,1,0:T(2,128)(2,1)S(1)}, u32[]{:S(2)}, u32[]{:S(2)}) async-start(bf16[64,8,2,1024]{3,2,1,0:T(2,128)(2,1)} %broadcast_in_dim.292), calls=%async_computation | async-start | bytes 4194304 | tf_op jit(solution)/shard_map/all_to_all | solution.py:30
  35.7 0.0 all-gather.2.cloned.1.call-start
  35.7 0.6 slice.494
  36.3 0.1 all-gather.2.cloned.1.call-update
  36.5 0.0 copy-done
  36.5 0.0 copy-start.2
  36.5 3.6 %gather_fusion.2 = s32[542]{0:T(1024)S(1)} fusion(s32[2048]{0:T(1024)S(1)} %copy-done, s32[1024]{0:T(1024)S(1)} %pad_clamp_fusion.1), kind=kCustom, calls=%fused_computation.1.clone | custom fusion | bytes 6504 | tf_op jit(solution)/shard_map/jit(_take)/gather | solution.py:72
  40.1 0.0 copy-done.2
  40.1 0.0 copy-start.1
  40.1 3.6 %gather_fusion.1 = s32[542]{0:T(1024)S(1)} fusion(s32[2048]{0:T(1024)S(1)} %copy-done.2, s32[1024]{0:T(1024)S(1)} %pad_clamp_fusion.1), kind=kCustom, calls=%fused_computation.clone | custom fusion | bytes 6504 | tf_op jit(solution)/shard_map/jit(_take)/gather | solution.py:73
  43.7 0.0 copy-done.1
  43.7 0.0 copy-start.3
  43.7 4.0 %gather_fusion = s32[542]{0:T(1024)S(1)} fusion(s32[512]{0:T(512)S(1)} %copy-done.1, s32[1024]{0:T(1024)S(1)} %pad_clamp_fusion), kind=kCustom, calls=%fused_computation.2 | custom fusion | bytes 6504 | tf_op jit(solution)/shard_map/jit(_take)/gather | solution.py:74
  47.7 0.0 copy-done.3
  47.7 0.0 copy-start.4
  47.7 0.2 convert_reduce_fusion
  47.9 0.4 fusion.2
  48.4 0.1 slice_convert_fusion.31
  48.4 0.1 slice_compare_fusion.29
  48.5 0.1 slice_compare_fusion.28
  48.6 0.1 slice_compare_fusion.27
  48.7 0.0 copy-done.4
  48.8 0.1 slice_convert_fusion.30
  48.8 33.7 %all-to-all-done = bf16[64,8,2,1024]{3,2,1,0:T(2,128)(2,1)S(1)} async-done(((bf16[64,8,2,1024]{3,2,1,0:T(2,128)(2,1)}), bf16[64,8,2,1024]{3,2,1,0:T(2,128)(2,1)S(1)}, u32[]{:S(2)}, u32[]{:S(2)}) %all-to-all-start) | async-done | bytes 2097184 | tf_op jit(solution)/shard_map/all_to_all | solution.py:30
  82.6 6.2 %broadcast_in_dim.293 = bf16[2,64,8,2,1024]{4,3,2,1,0:T(2,128)(2,1)} broadcast(bf16[64,8,2,1024]{3,2,1,0:T(2,128)(2,1)S(1)} %all-to-all-done), dimensions={1,2,3,4} | broadcast | bytes 6291456 | tf_op jit(solution)/shard_map/broadcast_in_dim | solution.py:31
  88.7 14.0 %all_to_all.10 = bf16[2,64,8,2,1024]{4,3,2,1,0:T(2,128)(2,1)S(1)} all-to-all(bf16[2,64,8,2,1024]{4,3,2,1,0:T(2,128)(2,1)} %broadcast_in_dim.293), channel_id=1, replica_groups=mesh['seq_0'=8,'seq_1'=8,'seq_2'=2,'grp'=4] {'seq_2'}, dimensions={0} | all-to-all | bytes 8388608 | tf_op jit(solution)/shard_map/all_to_all | solution.py:30
  102.7 5.9 %copy.11 = bf16[64,2,8,2,1024]{4,3,2,1,0:T(2,128)(2,1)} copy(bf16[64,2,8,2,1024]{4,3,2,0,1:T(2,128)(2,1)S(1)} %bitcast.43) | data formatting | bytes 8388608 | tf_op jit(solution)/shard_map/transpose | solution.py:44
  108.6 3.6 %copy.12 = bf16[128,8,2,1024]{3,1,2,0:T(8,128)(2,1)S(1)} copy(bf16[128,8,2,1024]{3,2,1,0:T(2,128)(2,1)} %bitcast.44) | data formatting | bytes 8388608
  112.3 0.0 copy-done.5
  112.3 2.5 %fusion.12 = f32[512,2048]{1,0:T(8,128)S(1)} fusion(bf16[1024,2048]{1,0:T(8,128)(2,1)S(1)} %bitcast.45, bf16[512,1024]{1,0:T(8,128)(2,1)S(1)} %copy-done.3, f32[1024]{0:T(1024)S(1)} %copy-done.5, f32[512]{0:T(512)S(1)} %add_rsqrt_fusion.1, f32[512]{0:T(512)S(1)} %broadcast_multiply_fusion.1), kind=kOutput, calls=%fused_computation.50 | convolution fusion | flops 2150105088 | bytes 9445376 | tf_op jit(solution)/shard_map/dot_general | solution.py:114
  114.7 0.6 fusion.11
  115.3 0.0 copy-start.6
  115.3 0.0 copy-start.7
  115.4 4.0 %collective-permute-start = (bf16[15,1024]{1,0:T(8,128)(2,1)S(1)}, bf16[15,1024]{1,0:T(8,128)(2,1)S(1)}, u32[]{:S(2)}, u32[]{:S(2)}) collective-permute-start(bf16[15,1024]{1,0:T(8,128)(2,1)S(1)} %get-tuple-element.11), channel_id=1, source_target_pairs={{0,1},{1,2},{2,3},{3,4},{4,5},{5,6},{6,7},{7,8},{8,9},{9,10},{10,1... | collective-permute-start | bytes 92168 | tf_op jit(solution)/shard_map/ppermute | solution.py:55
  119.3 2.1 %collective-permute-start.1 = (bf16[15,1024]{1,0:T(8,128)(2,1)S(1)}, bf16[15,1024]{1,0:T(8,128)(2,1)S(1)}, u32[]{:S(2)}, u32[]{:S(2)}) collective-permute-start(bf16[15,1024]{1,0:T(8,128)(2,1)S(1)} %get-tuple-element.12), channel_id=1, source_target_pairs={{1,0},{2,1},{3,2},{4,3},{5,4},{6,5},{7,6},{8,7},{9,8},{10,9},{11,1... | collective-permute-start | bytes 92168 | tf_op jit(solution)/shard_map/ppermute | solution.py:56
  121.5 0.1 slice_compare_fusion.26
  121.6 0.0 collective-permute-done
  121.6 7.6 %collective-permute-done.1 = bf16[15,1024]{1,0:T(8,128)(2,1)S(1)} collective-permute-done((bf16[15,1024]{1,0:T(8,128)(2,1)S(1)}, bf16[15,1024]{1,0:T(8,128)(2,1)S(1)}, u32[]{:S(2)}, u32[]{:S(2)}) %collective-permute-start.1) | collective-permute-done | bytes 30752 | tf_op jit(solution)/shard_map/ppermute | solution.py:56
  129.2 19.5 %fusion.64 = (f32[512]{0:T(512)S(1)}, f32[512]{0:T(512)S(1)}, f32[512,1024]{1,0:T(8,128)S(1)}) fusion(f32[1024]{0:T(1024)S(1)} %bitcast.57, bf16[15,1024]{1,0:T(8,128)(2,1)S(1)} %collective-permute-done.1, bf16[512,1024]{1,0:T(8,128)(2,1)S(1)} %fusion.11, pred[512]{0:T(512)(128)(4,1)S(1)} %get-tuple-element.73, f32[1024]{0:T(1024)S(1)} %bitcast.58, ...), kind=kLoop, calls=%fused_computation.200 | loop fusion | flops 112720896 | bytes 3353600 | tf_op jit(solution)/shard_map/reduce_sum | solution.py:138
  148.7 0.0 all-gather.2.cloned.1.call-done
  148.7 0.0 copy-done.6
  148.7 0.0 copy-done.7
  148.7 4.1 %fusion.5 = bf16[512,1024]{1,0:T(8,128)(2,1)} fusion(bf16[512,1024]{1,0:T(8,128)(2,1)S(1)} %copy-done.3, bf16[1024,1024]{0,1:T(8,128)(2,1)} %all-gather.2.cloned.1.call-done, f32[512,1024]{1,0:T(8,128)S(1)} %get-tuple-element.8, f32[1024]{0:T(1024)S(1)} %copy-done.6, f32[1024]{0:T(1024)S(1)} %copy-done.7, f32[512]{0:T(512)S(1)} %get-tuple-element.75, ...), kind=kOutput, calls=%fused_computation.39 | convolution fusion | flops 1080557568 | bytes 6305792 | tf_op jit(solution)/shard_map/dot_general | solution.py:140
  (13 shorter events, 0.2 us)
Async XLA Ops:
  6.5 29.9 %copy-start = (s32[2048]{0:T(1024)S(1)}, s32[2048]{0:T(1024)}, u32[]{:S(2)}) copy-start(s32[2048]{0:T(1024)} %param.19) | copy-start | bytes 24580
  20.3 62.2 %all-to-all-start = ((bf16[64,8,2,1024]{3,2,1,0:T(2,128)(2,1)}), bf16[64,8,2,1024]{3,2,1,0:T(2,128)(2,1)S(1)}, u32[]{:S(2)}, u32[]{:S(2)}) async-start(bf16[64,8,2,1024]{3,2,1,0:T(2,128)(2,1)} %broadcast_in_dim.292), calls=%async_computation | async-start | bytes 4194304 | tf_op jit(solution)/shard_map/all_to_all | solution.py:30
  35.7 113.0 %all-gather.2.cloned.1.call-start = ((), (), s32[]{:S(2)}) async-start(), calls=%async_computation.2 | async-start | bytes 2113536 | tf_op jit(solution)/shard_map/all_gather | solution.py:141
  36.5 3.6 %copy-start.2 = (s32[2048]{0:T(1024)S(1)}, s32[2048]{0:T(1024)}, u32[]{:S(2)}) copy-start(s32[2048]{0:T(1024)} %param.20) | copy-start | bytes 24580
  40.1 3.6 %copy-start.1 = (s32[512]{0:T(512)S(1)}, s32[512]{0:T(512)}, u32[]{:S(2)}) copy-start(s32[512]{0:T(512)} %param.21) | copy-start | bytes 6148
  43.7 4.0 %copy-start.3 = (bf16[512,1024]{1,0:T(8,128)(2,1)S(1)}, bf16[512,1024]{1,0:T(8,128)(2,1)}, u32[]{:S(2)}) copy-start(bf16[512,1024]{1,0:T(8,128)(2,1)} %param.12) | copy-start | bytes 3145732
  47.7 1.0 copy-start.4
  108.6 3.6 %copy-start.5 = (f32[1024]{0:T(1024)S(1)}, f32[1024]{0:T(1024)}, u32[]{:S(2)}) copy-start(f32[1024]{0:T(1024)} %param.13) | copy-start | bytes 12292
  115.3 33.4 %copy-start.6 = (f32[1024]{0:T(1024)S(1)}, f32[1024]{0:T(1024)}, u32[]{:S(2)}) copy-start(f32[1024]{0:T(1024)} %param.17) | copy-start | bytes 12292
  115.3 33.4 %copy-start.7 = (f32[1024]{0:T(1024)S(1)}, f32[1024]{0:T(1024)}, u32[]{:S(2)}) copy-start(f32[1024]{0:T(1024)} %param.16) | copy-start | bytes 12292
  115.4 6.2 %collective-permute-start = (bf16[15,1024]{1,0:T(8,128)(2,1)S(1)}, bf16[15,1024]{1,0:T(8,128)(2,1)S(1)}, u32[]{:S(2)}, u32[]{:S(2)}) collective-permute-start(bf16[15,1024]{1,0:T(8,128)(2,1)S(1)} %get-tuple-element.11), channel_id=1, source_target_pairs={{0,1},{1,2},{2,3},{3,4},{4,5},{5,6},{6,7},{7,8},{8,9},{9,10},{10,1... | collective-permute-start | bytes 92168 | tf_op jit(solution)/shard_map/ppermute | solution.py:55
  119.3 9.8 %collective-permute-start.1 = (bf16[15,1024]{1,0:T(8,128)(2,1)S(1)}, bf16[15,1024]{1,0:T(8,128)(2,1)S(1)}, u32[]{:S(2)}, u32[]{:S(2)}) collective-permute-start(bf16[15,1024]{1,0:T(8,128)(2,1)S(1)} %get-tuple-element.12), channel_id=1, source_target_pairs={{1,0},{2,1},{3,2},{4,3},{5,4},{6,5},{7,6},{8,7},{9,8},{10,9},{11,1... | collective-permute-start | bytes 92168 | tf_op jit(solution)/shard_map/ppermute | solution.py:56
Sparse Core Ops, SparseCore 0:
  39.7 102.1 all-gather.1
where the time goes:
time: 160 us
  waiting for transfers between devices  41.4 us (26%)
  local copies, waits for them, and re-layouts  31.6 us (20%)
  blocking collectives  23 us (14%)
  other arithmetic  21.9 us (14%)
  starting transfers between devices  21.5 us (13%)
  between operations  13.7 us (9%)
  matrix products  6.58 us (4%)
    all_to_all x1, waiting for transfers between devices, sent_to_all(): lax.all_to_all(jnp.broadcast_to(array[None], (size, *array.shape)), axis,...  33.7 us
    reduce_sum x1, other arithmetic, per_device(): jnp.sum(mixed, axis=1)  19.5 us
    all_to_all x1, starting transfers between devices, sent_to_all(): lax.all_to_all(jnp.broadcast_to(array[None], (size, *array.shape)), axis,...  15.3 us
    all_to_all x1, blocking collectives, sent_to_all(): lax.all_to_all(jnp.broadcast_to(array[None], (size, *array.shape)), axis,...  14 us
    broadcast_in_dim x2, local copies, waits for them, and re-layouts, sent_to_all(): jnp.broadcast_to(array[None], (size, *array.shape))  9.51 us
    all_gather x1, blocking collectives, turned_gather(): lax.all_gather(both, axis, axis=0, tiled=True)  9.01 us
    ppermute x1, waiting for transfers between devices, extended(): lax.ppermute(leading, axis, [(b, a) for a, b in up])  7.61 us
    transpose x1, local copies, waits for them, and re-layouts, gather_axes(): return joined_along(pieces.swapaxes(0, 1).reshape(-1, *array.shape), dim)  5.93 us
  transfers between devices with their start and end apart: 4, of which 2 were waited for; matrix products, arithmetic and copies ran while one was open for 32% of the time, Pallas kernels for 0%

commit v1 on v0

v1 whole, which is shorter than its diff:
```python
import jax
import jax.numpy as jnp
from jax import lax
from jax.experimental import pallas as pl
from jax.experimental.pallas import tpu as pltpu
from jax.sharding import Mesh
from jax.sharding import PartitionSpec as P

D = 1024
KER = 31
BLK = 128
EDGE = 16
WIN = BLK + 2 * EDGE
Z, YH, YL, C, X = 8, 4, 2, 2, 4
PART = D // X
ALL = ("z", "yh", "yl", "c", "x")
SEQ = ("z", "yh", "yl", "c")
epsilon = 1e-05


def sent_to_all(array, axes):
    size = lax.axis_size(axes)
    return lax.all_to_all(
        jnp.broadcast_to(array[None], (size, *array.shape)), axes, 0, 0, tiled=True
    )


def sigmoid(v):
    return 0.5 * jnp.tanh(0.5 * v) + 0.5


def normed_rows(rows, gain):
    values = rows.astype(jnp.float32)
    centered = values - jnp.mean(values, axis=1, keepdims=True)
    spread = jnp.mean(centered * centered, axis=1, keepdims=True)
    return (centered * lax.rsqrt(spread + epsilon) * gain).astype(jnp.bfloat16)


def module_kernel(
    place, utts, offs, lens, low_ref, frames_ref, high_ref, gain1_ref, taps_ref, gain2_ref, bias2_ref, own_ref,
    other_ref, out_ref, w_ref, normed_ref, gated_ref, mixed_ref, act_ref, taps32_ref, sems,
):
    rows = frames_ref.shape[0]
    blocks = rows // BLK
    core = place[1]

    def copies(x):
        found = []
        for source, half in ((own_ref, core), (other_ref, 1 - core)):
            for yl in range(YL):
                for yh in range(YH):
                    at = pl.multiple_of((yh * YL + yl) * (C * 8) + half * 8, 8)
                    found.append(
                        pltpu.make_async_copy(
                            source.at[yl, x, yh], w_ref.at[x, :, pl.ds(at, 8), :], sems.at[x]
                        )
                    )
        return found

    for x in range(X):
        for copy in copies(x):
            copy.start()

    gain1 = gain1_ref[...]
    normed_ref[:EDGE] = normed_rows(low_ref[...], gain1)
    for b in range(blocks):
        normed_ref[EDGE + b * BLK : EDGE + (b + 1) * BLK] = normed_rows(
            frames_ref[b * BLK : (b + 1) * BLK], gain1
        )
    normed_ref[EDGE + rows :] = normed_rows(high_ref[...], gain1)
    taps32_ref[...] = taps_ref[...].astype(jnp.float32)

    limits, firsts = [], []
    for b in range(blocks):
        at = place[0] + b
        off = offs[at]
        limits.append(lens[utts[at]] - off * BLK)
        firsts.append(jnp.where(off == 0, EDGE, 0))
    places = lax.broadcasted_iota(jnp.int32, (WIN, BLK), 0)

    for x in range(X):
        for copy in copies(x):
            copy.wait()
        w_v = w_ref[x, :, :, 0:PART].reshape(D, PART)
        w_g = w_ref[x, :, :, PART : 2 * PART].reshape(D, PART)
        values = jnp.dot(normed_ref[...], w_v, preferred_element_type=jnp.float32)
        gates = jnp.dot(normed_ref[...], w_g, preferred_element_type=jnp.float32)
        gated = (values * sigmoid(gates)).astype(jnp.bfloat16).astype(jnp.float32)
        for b in range(blocks):
            keep = (places >= firsts[b]) & (places < limits[b] + EDGE)
            for part in range(PART // 128):
                gated_ref[x * (PART // 128) + part, b] = jnp.where(
                    keep, gated[b * BLK : b * BLK + WIN, part * 128 : (part + 1) * 128], 0.0
                )

    def mix(step, carry):
        col, b = step // blocks, step % blocks
        lane = pl.multiple_of(col * 128, 128)
        total = jnp.zeros((BLK, 128), jnp.float32)
        for shift in range(8):
            window = gated_ref[col, b, pl.ds(shift, BLK + 24), :]
            for coarse in range(4):
                tap = 8 * coarse + shift - 1
                if tap >= 0:
                    total = total + window[8 * coarse : 8 * coarse + BLK] * taps32_ref[tap : tap + 1, pl.ds(lane, 128)]
        mixed_ref[col, b] = total
        return carry

    lax.fori_loop(0, (D // 128) * blocks, mix, 0)

    def settle(step, carry):
        b = step // 2
        half = pl.multiple_of((step % 2) * 64, 64)
        at = pl.multiple_of(step * 64, 64)
        first = mixed_ref[0, b, pl.ds(half, 64), :]
        total, squares = first, first * first
        for col in range(1, D // 128):
            piece = mixed_ref[col, b, pl.ds(half, 64), :]
            total = total + piece
            squares = squares + piece * piece
        average = jnp.sum(total, axis=1, keepdims=True) / float(D)
        spread = jnp.sum(squares, axis=1, keepdims=True) / float(D) - average * average
        scale = lax.rsqrt(spread + epsilon)
        for col in range(D // 128):
            lanes = slice(col * 128, (col + 1) * 128)
            piece = mixed_ref[col, b, pl.ds(half, 64), :]
            y = (piece - average) * scale * gain2_ref[:, lanes] + bias2_ref[:, lanes]
            act_ref[pl.ds(at, 64), lanes] = (y * sigmoid(y)).astype(jnp.bfloat16)
        return carry

    lax.fori_loop(0, rows // 64, settle, 0)

    per = D // X
    for n in range(X):
        output = jnp.zeros((rows, per), jnp.float32)
        for x in range(X):
            w_o = w_ref[x, 2 * n : 2 * n + 2, :, 2 * PART :].reshape(per, PART)
            output = output + lax.dot_general(
                act_ref[:, x * PART : (x + 1) * PART], w_o, (((1,), (1,)), ((), ())),
                preferred_element_type=jnp.float32,
            )
        lanes = slice(n * per, (n + 1) * per)
        for b in range(blocks):
            here = slice(b * BLK, (b + 1) * BLK)
            alive = lax.broadcasted_iota(jnp.int32, (BLK, per), 0) < limits[b]
            out_ref[here, lanes] = (
                frames_ref[here, lanes].astype(jnp.float32) + jnp.where(alive, output[here], 0.0)
            ).astype(jnp.bfloat16)


def per_device(
    frames, ln1_gain, w_in, w_dw, ln2_gain, ln2_bias, w_out, block_utt, block_off, lengths
):
    rows = frames.shape[0]
    count = lax.axis_size(ALL)
    up = [(i, i + 1) for i in range(count - 1)]
    low = lax.ppermute(frames[rows - EDGE :], ALL, up)
    high = lax.ppermute(frames[:EDGE], ALL, [(b, a) for a, b in up])

    held = jnp.concatenate([w_in.reshape(8, 2 * PART), w_out.T], axis=1)
    for axes in (("z",), ("yh",), ("yl", "x")):
        held = sent_to_all(held, axes)
        held = held.reshape(-1, *held.shape[-2:])
    held = held.reshape(YL, X, YH, Z, 8, 3 * PART)
    other = lax.ppermute(held, "c", [(0, 1), (1, 0)])

    place = jnp.stack([lax.axis_index(ALL) * (rows // BLK), lax.axis_index("c")]).astype(jnp.int32)
    vmem = pl.BlockSpec(memory_space=pltpu.VMEM)
    hbm = pl.BlockSpec(memory_space=pl.ANY)
    blocks = rows // BLK
    return pl.pallas_call(
        module_kernel,
        name="module",
        out_shape=jax.ShapeDtypeStruct((rows, D), jnp.bfloat16),
        grid_spec=pltpu.PrefetchScalarGridSpec(
            num_scalar_prefetch=4,
            grid=(),
            in_specs=[vmem] * 7 + [hbm] * 2,
            out_specs=vmem,
            scratch_shapes=[
                pltpu.VMEM((X, Z, YH * YL * C * 8, 3 * PART), jnp.bfloat16),
                pltpu.VMEM((rows + 2 * EDGE, D), jnp.bfloat16),
                pltpu.VMEM((D // 128, blocks, WIN, 128), jnp.float32),
                pltpu.VMEM((D // 128, blocks, BLK, 128), jnp.float32),
                pltpu.VMEM((rows, D), jnp.bfloat16),
                pltpu.VMEM((KER, D), jnp.float32),
                pltpu.SemaphoreType.DMA((X,)),
            ],
        ),
        compiler_params=pltpu.CompilerParams(vmem_limit_bytes=48 * 1024 * 1024),
        cost_estimate=pl.CostEstimate(flops=3 * 2 * rows * D * D, bytes_accessed=8 * 2**20, transcendentals=rows * D * 2),
    )(
        place, block_utt, block_off, lengths, low, frames, high, ln1_gain[None], w_dw, ln2_gain[None],
        ln2_bias[None], held, other,
    )


def solution(mesh):
    finer = Mesh(mesh.devices.reshape(Z, YH, YL, C, X), ALL)
    in_specs = (
        P(ALL, None), P(), P(SEQ, None, "x"), P(), P(), P(), P("x", SEQ), P(), P(), P(),
    )
    return jax.shard_map(
        per_device, mesh=finer, in_specs=in_specs, out_specs=P(ALL, None), check_vma=False
    )
```

time: 160 us -> 111 us (0.69)
  the two profiles are of different devices: /device:TPU:63 before, /device:TPU:64 now
where the time goes in v1:
time: 111 us
  blocking collectives  75.5 us (68%)
  Pallas kernels  14.2 us (13%)
  starting transfers between devices  9.91 us (9%)
  waiting for transfers between devices  7.44 us (7%)
  local copies, waits for them, and re-layouts  2.99 us (3%)
    all_to_all x3, blocking collectives, sent_to_all(): lax.all_to_all(jnp.broadcast_to(array[None], (size, *array.shape)), axes,...  75.5 us
    pallas_call x1, Pallas kernels, per_device(): pl.pallas_call(module_kernel, name='module', out_shape=jax.ShapeDtypeStru...  14.2 us
    ppermute x1, waiting for transfers between devices, per_device(): low = lax.ppermute(frames[rows - EDGE:], ALL, up)  7.43 us
    ppermute x1, starting transfers between devices, per_device(): high = lax.ppermute(frames[:EDGE], ALL, [(b, a) for a, b in up])  6.08 us
  transfers between devices with their start and end apart: 3, of which 1 were waited for; matrix products, arithmetic and copies ran while one was open for 1% of the time, Pallas kernels for 0%

profile of v1, /device:TPU:64, one launch (start us, length us, event | category | flops | bytes accessed | tf_op | source)
XLA Modules:
  0.0 110.9 jit_solution(1293253250453676157)
XLA Ops:
  0.0 0.7 copy.11
  0.7 0.7 pad_maximum_fusion
  1.4 16.9 %all_to_all.15 = bf16[8,8,768]{2,1,0:T(8,128)(2,1)S(1)} all-to-all(bf16[8,8,768]{2,1,0:T(8,128)(2,1)S(1)} %broadcast_in_dim.31), channel_id=1, replica_groups=mesh['z'=8,'yh'=4,'yl'=2,'c'=2,'x'=4] {'z'}, dimensions={0} | all-to-all | bytes 196608 | tf_op jit(solution)/shard_map/all_to_all | solution.py:23
  18.3 19.1 %all_to_all.16 = bf16[4,8,8,768]{3,2,1,0:T(8,128)(2,1)S(1)} all-to-all(bf16[4,8,8,768]{3,2,1,0:T(8,128)(2,1)S(1)} %broadcast_in_dim.32), channel_id=1, replica_groups=mesh['z'=8,'yh'=4,'yl'=2,'c'=2,'x'=4] {'yh'}, dimensions={0} | all-to-all | bytes 786432 | tf_op jit(solution)/shard_map/all_to_all | solution.py:23
  37.4 0.2 broadcast_in_dim.34
  37.6 0.0 copy-start.1
  37.7 0.0 copy-start.2
  37.7 0.0 copy-start.3
  37.7 0.0 copy-start.4
  37.7 0.0 copy-start.5
  37.7 0.0 copy-start.6
  37.7 0.0 copy-start.7
  37.7 39.5 %all_to_all.17 = bf16[8,32,8,768]{3,2,1,0:T(8,128)(2,1)S(1)} all-to-all(bf16[8,32,8,768]{3,2,1,0:T(8,128)(2,1)S(1)} %broadcast_in_dim.34), channel_id=1, replica_groups=mesh['z'=8,'yh'=4,'yl'=2,'c'=2,'x'=4] {'yl','x'}, dimensions={0} | all-to-all | bytes 6291456 | tf_op jit(solution)/shard_map/all_to_all | solution.py:23
  77.2 1.9 %collective-permute-start.2 = (bf16[2,4,4,8,8,768]{5,4,3,2,1,0:T(8,128)(2,1)S(1)}, bf16[2,4,4,8,8,768]{5,4,3,2,1,0:T(8,128)(2,1)}, u32[]{:S(2)}, u32[]{:S(2)}) collective-permute-start(bf16[2,4,4,8,8,768]{5,4,3,2,1,0:T(8,128)(2,1)S(1)} %bitcast.10), channel_id=1, source_target_pairs={{0,4},{4,0},{1,5},{5,1},{2,6},{6,2},{3,7},{7,3},{8,12},{12,8},{9,1... | collective-permute-start | bytes 9437192 | tf_op jit(solution)/shard_map/ppermute | solution.py:165
  79.1 0.8 fusion
  79.9 6.1 %collective-permute-start.1 = (bf16[16,1024]{1,0:T(8,128)(2,1)S(1)}, bf16[16,1024]{1,0:T(8,128)(2,1)S(1)}, u32[]{:S(2)}, u32[]{:S(2)}) collective-permute-start(bf16[16,1024]{1,0:T(8,128)(2,1)S(1)} %get-tuple-element.5), channel_id=1, source_target_pairs={{1,0},{2,1},{3,2},{4,3},{5,4},{6,5},{7,6},{8,7},{9,8},{10,9},{11,1... | collective-permute-start | bytes 98312 | tf_op jit(solution)/shard_map/ppermute | solution.py:158
  86.0 1.9 %collective-permute-start = (bf16[16,1024]{1,0:T(8,128)(2,1)S(1)}, bf16[16,1024]{1,0:T(8,128)(2,1)S(1)}, u32[]{:S(2)}, u32[]{:S(2)}) collective-permute-start(bf16[16,1024]{1,0:T(8,128)(2,1)S(1)} %get-tuple-element.6), channel_id=1, source_target_pairs={{0,1},{1,2},{2,3},{3,4},{4,5},{5,6},{6,7},{7,8},{8,9},{9,10},{10,1... | collective-permute-start | bytes 98312 | tf_op jit(solution)/shard_map/ppermute | solution.py:157
  87.9 0.1 pad_add_fusion.place
  88.0 0.0 collective-permute-done.1.high_ref
  88.0 7.4 %collective-permute-done.low_ref = bf16[16,1024]{1,0:T(8,128)(2,1)S(1)} collective-permute-done((bf16[16,1024]{1,0:T(8,128)(2,1)S(1)}, bf16[16,1024]{1,0:T(8,128)(2,1)S(1)}, u32[]{:S(2)}, u32[]{:S(2)}) %collective-permute-start) | collective-permute-done | bytes 32800 | tf_op jit(solution)/shard_map/ppermute | solution.py:157
  95.5 0.0 collective-permute-done.2.other_ref
  95.5 0.0 copy-done.1
  95.5 0.0 copy-done.2
  95.5 0.0 copy-done.3
  95.5 0.0 copy-done.4
  95.5 0.0 copy-done.5
  95.5 0.0 copy-done.6
  95.5 0.0 copy-done.7
  95.5 0.0 copy-start
  95.5 1.2 %copy-done = bf16[512,1024]{1,0:T(8,128)(2,1)S(1)} copy-done((bf16[512,1024]{1,0:T(8,128)(2,1)S(1)}, bf16[512,1024]{1,0:T(8,128)(2,1)}, u32[]{:S(2)}) %copy-start) | copy-done | bytes 1048600
  96.7 14.2 %module.1 = bf16[512,1024]{1,0:T(8,128)(2,1)} custom-call(s32[2]{0:T(128)S(1)} %pad_add_fusion.place, s32[2048]{0:T(1024)S(1)} %copy-done.2, s32[2048]{0:T(1024)S(1)} %copy-done.3, s32[512]{0:T(512)S(1)} %copy-done.7, bf16[16,1024]{1,0:T(8,128)(2,1)S(1)} %collective-permute-done.low_ref, bf16[512,1024]{1,0:T(8,128)(2,1)S(1)} %copy-done, ...), custom_call_target="tpu_custom_call" | custom-call | flops 3221225472 | bytes 8388608 | tf_op jit(solution)/shard_map/module/pallas_call | solution.py:171
  (2 shorter events, 0.0 us)
Async XLA Ops:
  37.6 57.8 %copy-start.1 = (bf16[31,1024]{1,0:T(8,128)(2,1)S(1)}, bf16[31,1024]{1,0:T(8,128)(2,1)}, u32[]{:S(2)}) copy-start(bf16[31,1024]{1,0:T(8,128)(2,1)} %taps_ref.1) | copy-start | bytes 190468
  37.7 57.8 %copy-start.2 = (s32[2048]{0:T(1024)S(1)}, s32[2048]{0:T(1024)}, u32[]{:S(2)}) copy-start(s32[2048]{0:T(1024)} %utts.1) | copy-start | bytes 24580
  37.7 57.8 %copy-start.3 = (s32[2048]{0:T(1024)S(1)}, s32[2048]{0:T(1024)}, u32[]{:S(2)}) copy-start(s32[2048]{0:T(1024)} %offs.1) | copy-start | bytes 24580
  37.7 57.8 %copy-start.4 = (f32[1024]{0:T(1024)S(1)}, f32[1024]{0:T(1024)}, u32[]{:S(2)}) copy-start(f32[1024]{0:T(1024)} %param.11) | copy-start | bytes 12292
  37.7 57.8 %copy-start.5 = (f32[1024]{0:T(1024)S(1)}, f32[1024]{0:T(1024)}, u32[]{:S(2)}) copy-start(f32[1024]{0:T(1024)} %param.14) | copy-start | bytes 12292
  37.7 57.8 %copy-start.6 = (f32[1024]{0:T(1024)S(1)}, f32[1024]{0:T(1024)}, u32[]{:S(2)}) copy-start(f32[1024]{0:T(1024)} %param.15) | copy-start | bytes 12292
  37.7 57.8 %copy-start.7 = (s32[512]{0:T(512)S(1)}, s32[512]{0:T(512)}, u32[]{:S(2)}) copy-start(s32[512]{0:T(512)} %lens.1) | copy-start | bytes 6148
  77.2 18.2 %collective-permute-start.2 = (bf16[2,4,4,8,8,768]{5,4,3,2,1,0:T(8,128)(2,1)S(1)}, bf16[2,4,4,8,8,768]{5,4,3,2,1,0:T(8,128)(2,1)}, u32[]{:S(2)}, u32[]{:S(2)}) collective-permute-start(bf16[2,4,4,8,8,768]{5,4,3,2,1,0:T(8,128)(2,1)S(1)} %bitcast.10), channel_id=1, source_target_pairs={{0,4},{4,0},{1,5},{5,1},{2,6},{6,2},{3,7},{7,3},{8,12},{12,8},{9,1... | collective-permute-start | bytes 9437192 | tf_op jit(solution)/shard_map/ppermute | solution.py:165
  79.9 8.1 %collective-permute-start.1 = (bf16[16,1024]{1,0:T(8,128)(2,1)S(1)}, bf16[16,1024]{1,0:T(8,128)(2,1)S(1)}, u32[]{:S(2)}, u32[]{:S(2)}) collective-permute-start(bf16[16,1024]{1,0:T(8,128)(2,1)S(1)} %get-tuple-element.5), channel_id=1, source_target_pairs={{1,0},{2,1},{3,2},{4,3},{5,4},{6,5},{7,6},{8,7},{9,8},{10,9},{11,1... | collective-permute-start | bytes 98312 | tf_op jit(solution)/shard_map/ppermute | solution.py:158
  86.0 9.5 %collective-permute-start = (bf16[16,1024]{1,0:T(8,128)(2,1)S(1)}, bf16[16,1024]{1,0:T(8,128)(2,1)S(1)}, u32[]{:S(2)}, u32[]{:S(2)}) collective-permute-start(bf16[16,1024]{1,0:T(8,128)(2,1)S(1)} %get-tuple-element.6), channel_id=1, source_target_pairs={{0,1},{1,2},{2,3},{3,4},{4,5},{5,6},{6,7},{7,8},{8,9},{9,10},{10,1... | collective-permute-start | bytes 98312 | tf_op jit(solution)/shard_map/ppermute | solution.py:157
  95.5 1.2 %copy-start = (bf16[512,1024]{1,0:T(8,128)(2,1)S(1)}, bf16[512,1024]{1,0:T(8,128)(2,1)}, u32[]{:S(2)}) copy-start(bf16[512,1024]{1,0:T(8,128)(2,1)} %frames_ref.1) | copy-start | bytes 3145732
